TPU v7x, 32 devices: a whole 2x2x4 slice. The times are simulated.
32 devices in a mesh: loop: 4 (over y, core), inner: 8 (over z, x).
Axes of the slice: x: 2, y: 2, z: 4, core: 2. Of those that a mesh axis runs over, the one named last changes fastest.
Arguments:
- snapshots: bfloat16 [8192, 1024], P(('loop', 'inner')), may hold values from -6 to 6
- bins: int32 [8192], replicated, may hold values from 0 to 63, as said below
- pairs: int32 [256, 2], replicated, may hold values from 0 to 63, as said below
- start_weights: bfloat16 [1024, 32], replicated, may hold values from -0.1875 to 0.1875
Outputs:
- basis: float32 [8192, 96], P(('loop', 'inner'))
- coefficients: float32 [4, 32, 32], replicated
Inputs may be any that keep to these rules, and one draw needn't show every extreme that they name: `bins`: the snapshot in row n has a bin in [r * 8, (r + 1) * 8), where r = (n // 256) mod (8). `pairs`: every row (a, b) has a <= b <= a + 8; every bin is paired with itself.
All inputs are finite; a program needn't handle non-finite values.
Results may differ from a plain program's by a relative error of at most 0.0003.
Values may be sent and summed in bfloat16 or wider, within the bound.
No kernel may reach another device: no remote copies, remote signals or barrier semaphores. Data moves between devices by JAX's collectives and lax.ppermute only.
A program may use at most 64 MiB of HBM per device.

v0:
```python
import jax
import jax.numpy as jnp
from jax import lax
from jax.sharding import PartitionSpec as P

STEPS = 2
BINS_COL = 8


def extended(cells, sides, width):
    for axis, dim in sides:
        count = lax.axis_size(axis)
        ends = count - 1
        head = lax.slice_in_dim(cells, 0, width, axis=dim)
        tail = lax.slice_in_dim(cells, cells.shape[dim] - width, cells.shape[dim], axis=dim)
        cells = jnp.concatenate(
            [
                lax.ppermute(tail, axis, [(i, (i + 1) % count) for i in range(ends)]),
                cells,
                lax.ppermute(head, axis, [((i + 1) % count, i) for i in range(ends)]),
            ],
            axis=dim,
        )
    return cells


def matches(values, targets):
    return (values[:, None] == targets[None, :]).astype(jnp.float32)


def local_gram(left, right):
    return jnp.dot(left.T, right, precision=lax.Precision.HIGHEST)


def finish(matrix, gram_total):
    lower_factor = jnp.linalg.cholesky(gram_total)
    result = lax.linalg.triangular_solve(
        lower_factor, matrix, left_side=False, lower=True, transpose_a=True
    )
    return (result, lower_factor.T)


def local(snapshots, bins, pairs, start_weights):
    row_count, features = snapshots.shape
    block_width = start_weights.shape[1]
    n_loop = lax.axis_size("loop")
    n_inner = lax.axis_size("inner")
    column = lax.axis_index("inner")
    group = lax.axis_index("loop")
    bin_grid = jnp.pad(
        bins.reshape(n_loop, n_inner, row_count), ((0, 0), (1, 1), (0, 0)), constant_values=-1
    )
    side_rows = extended(snapshots, (("inner", 0),), row_count)
    partner_rows = lax.all_gather(side_rows[None], "loop", axis=0, tiled=True)
    tile_rows = partner_rows.reshape(n_loop * 3 * row_count, features)
    tile_bins = lax.dynamic_slice_in_dim(bin_grid, column, 3, 1).reshape(-1)
    my_bins = lax.dynamic_slice_in_dim(bins, (group * n_inner + column) * row_count, row_count)
    bin_base = column * BINS_COL
    my_ids = bin_base + jnp.arange(BINS_COL, dtype=jnp.int32)
    window_ids = bin_base - BINS_COL + jnp.arange(3 * BINS_COL, dtype=jnp.int32)
    left_bins = pairs[:, 0]
    right_bins = pairs[:, 1]
    pair_count = jnp.dot(
        matches(left_bins, my_ids).T,
        matches(right_bins, window_ids),
        precision=lax.Precision.HIGHEST,
    )
    pair_count = pair_count + jnp.dot(
        matches(right_bins, my_ids).T,
        matches(left_bins, window_ids),
        precision=lax.Precision.HIGHEST,
    )
    linked_bins = jnp.where(pair_count > 0.5, 1.0, 0.0).astype(jnp.float32)
    my_hot = matches(my_bins, my_ids)
    row_links = jnp.dot(my_hot, linked_bins)
    mine_wide = snapshots.astype(jnp.float32)
    mine_norms = jnp.sum(mine_wide * mine_wide, axis=1)
    epsilon = features / 3.0
    part_hot = matches(tile_bins, window_ids) * (tile_bins >= 0).astype(jnp.float32)[:, None]
    band_mask = jnp.dot(row_links, part_hot.T)
    part_wide = tile_rows.astype(jnp.float32)
    part_norms = jnp.sum(part_wide * part_wide, axis=1)
    products = lax.dot_general(
        snapshots, tile_rows, (((1,), (1,)), ((), ())), preferred_element_type=jnp.float32
    )
    distance = mine_norms[:, None] + part_norms[None, :] - 2.0 * products
    kept_tiles = [band_mask * jnp.exp(-distance / epsilon)]

    def current_kernel(which):
        return kept_tiles[which]

    degree = jnp.sum(current_kernel(0), axis=1)
    inv_root = lax.rsqrt(degree)
    start_block = jnp.dot(snapshots, start_weights, preferred_element_type=jnp.float32)
    start_total = lax.psum(local_gram(start_block, start_block), ("loop", "inner"))
    current, unused = finish(start_block, start_total)
    basis_blocks = [current]
    coefficients = []
    previous = current
    prev_b = jnp.zeros((block_width, block_width), jnp.float32)
    for lanczos_step in range(STEPS):
        scaled = inv_root[:, None] * current
        vec_side = extended(scaled, (("inner", 0),), row_count)
        vec_strip = lax.all_gather(vec_side[None], "loop", axis=0, tiled=True)
        strip = vec_strip.reshape(n_loop * 3 * row_count, block_width)
        total = jnp.dot(current_kernel(0), strip, precision=lax.Precision.HIGHEST)
        image = inv_root[:, None] * total
        projected = lax.psum(local_gram(current, image), ("loop", "inner"))
        image = image - jnp.dot(current, projected, precision=lax.Precision.HIGHEST)
        if lanczos_step > 0:
            image = image - jnp.dot(previous, prev_b.T, precision=lax.Precision.HIGHEST)
        gram_total = lax.psum(local_gram(image, image), ("loop", "inner"))
        following, factor = finish(image, gram_total)
        coefficients.append(projected)
        coefficients.append(factor)
        previous = current
        prev_b = factor
        current = following
        basis_blocks.append(current)
    return (jnp.concatenate(basis_blocks, axis=1), jnp.stack(coefficients))


def solution(mesh):
    in_specs = (P(("loop", "inner"), None), P(), P(), P())
    out_specs = (P(("loop", "inner"), None), P())
    return jax.shard_map(local, mesh=mesh, in_specs=in_specs, out_specs=out_specs, check_vma=False)
```

profile of v0, /device:TPU:0, one launch (start us, length us, event | category | flops | bytes accessed | tf_op | source)
XLA Modules:
  0.0 321.3 jit_solution(17234646396150438926)
XLA Ops:
  7.3 1.4 collective-permute-start.1
  8.7 5.5 %collective-permute-start = (bf16[256,1024]{1,0:T(8,128)(2,1)}, bf16[256,1024]{1,0:T(8,128)(2,1)S(1)}, u32[]{:S(2)}, u32[]{:S(2)}) collective-permute-start(bf16[256,1024]{1,0:T(8,128)(2,1)} %param.7), channel_id=1, source_target_pairs={{0,1},{1,2},{2,3},{3,4},{4,5},{5,6},{6,7},{8,9},{9,10},{10,11},{11... | collective-permute-start | bytes 1572872 | tf_op jit(solution)/shard_map/ppermute | solution.py:18
  14.2 10.2 %collective-permute-done.1 = bf16[256,1024]{1,0:T(8,128)(2,1)S(1)} collective-permute-done((bf16[256,1024]{1,0:T(8,128)(2,1)}, bf16[256,1024]{1,0:T(8,128)(2,1)S(1)}, u32[]{:S(2)}, u32[]{:S(2)}) %collective-permute-start.1) | collective-permute-done | bytes 524320 | tf_op jit(solution)/shard_map/ppermute | solution.py:20
  24.4 11.5 %collective-permute-done = bf16[256,1024]{1,0:T(8,128)(2,1)S(1)} collective-permute-done((bf16[256,1024]{1,0:T(8,128)(2,1)}, bf16[256,1024]{1,0:T(8,128)(2,1)S(1)}, u32[]{:S(2)}, u32[]{:S(2)}) %collective-permute-start) | collective-permute-done | bytes 524320 | tf_op jit(solution)/shard_map/ppermute | solution.py:18
  35.9 2.3 pad_maximum_fusion
  38.4 0.2 fusion.55
  38.6 0.2 fusion.56
  38.8 42.3 %psum.35 = f32[32,32]{0,1:T(8,128)S(1)} all-reduce(f32[32,32]{0,1:T(8,128)S(1)} %fusion.56), channel_id=1, replica_groups=mesh['loop'=4,'inner'=8] {'loop','inner'}, use_global_device_ids=true, to_apply=%region_0.1 | all-reduce | flops 1024 | bytes 8192 | tf_op jit(solution)/shard_map/psum | solution.py:95
  81.2 2.9 cholesky.59
  84.1 0.6 compare_reduce_fusion.2
  84.8 0.7 fusion.35
  85.4 2.4 custom-call.7
  87.9 0.2 multiply_reduce_fusion.1
  88.1 0.3 fusion.20
  88.4 0.3 fusion.9
  88.7 4.2 %multiply_reduce_fusion = f32[3072]{0:T(1024)S(1)} fusion(bf16[3072,1024]{1,0:T(8,128)(2,1)} %all-gather.5.cloned.1.call-done), kind=kLoop, calls=%fused_computation | loop fusion | flops 9434112 | bytes 6303744 | tf_op jit(solution)/shard_map/reduce_sum | solution.py:82
  92.9 0.4 copy-done.1
  93.3 4.0 %fusion.4 = f32[256,3072]{1,0:T(8,128)} fusion(bf16[3072,1024]{1,0:T(8,128)(2,1)S(1)} %copy-done.1, bf16[256,1024]{1,0:T(8,128)(2,1)S(1)} %copy-done.2, f32[3072]{0:T(1024)S(1)} %multiply_reduce_fusion, f32[256]{0:T(256)S(1)} %multiply_reduce_fusion.1), kind=kOutput, calls=%fused_computation.7 | convolution fusion | flops 1614544896 | bytes 9974784 | tf_op jit(solution)/shard_map/dot_general | solution.py:83
  97.3 2.8 fusion.52
  100.1 0.2 broadcast_multiply_fusion.1
  100.3 1.3 collective-permute-start.3
  101.6 4.8 %collective-permute-start.2 = (f32[256,32]{0,1:T(8,128)S(1)}, f32[256,32]{0,1:T(8,128)S(1)}, u32[]{:S(2)}, u32[]{:S(2)}) collective-permute-start(f32[256,32]{0,1:T(8,128)S(1)} %get-tuple-element.18), channel_id=1, source_target_pairs={{0,1},{1,2},{2,3},{3,4},{4,5},{5,6},{6,7},{8,9},{9,10},{10,11},{11... | collective-permute-start | bytes 98312 | tf_op jit(solution)/shard_map/ppermute | solution.py:18
  106.4 1.6 collective-permute-done.2
  108.0 7.2 %all-gather.1 = f32[3072,32]{0,1:T(8,128)S(1)} all-gather(f32[768,32]{0,1:T(8,128)S(1)} %pad_maximum_fusion.1), channel_id=3, replica_groups=mesh['loop'=4,'inner'=8] {'loop'}, dimensions={0}, use_global_device_ids=true | all-gather | bytes 491520 | tf_op jit(solution)/shard_map/all_gather | solution.py:104
  115.2 2.8 convolution_multiply_fusion.3
  118.1 41.4 %psum.36 = f32[32,32]{0,1:T(8,128)S(1)} all-reduce(f32[32,32]{0,1:T(8,128)S(1)} %fusion.57), channel_id=1, replica_groups=mesh['loop'=4,'inner'=8] {'loop','inner'}, use_global_device_ids=true, to_apply=%region_6.9 | all-reduce | flops 1024 | bytes 8192 | tf_op jit(solution)/shard_map/psum | solution.py:108
  159.7 0.2 fusion.58
  159.9 39.5 %psum.37 = f32[32,32]{0,1:T(8,128)S(1)} all-reduce(f32[32,32]{0,1:T(8,128)S(1)} %fusion.58), channel_id=1, replica_groups=mesh['loop'=4,'inner'=8] {'loop','inner'}, use_global_device_ids=true, to_apply=%region_7.10 | all-reduce | flops 1024 | bytes 8192 | tf_op jit(solution)/shard_map/psum | solution.py:112
  199.4 2.9 cholesky.70
  202.4 0.6 compare_reduce_fusion.1
  203.0 0.7 fusion.43
  203.7 2.4 custom-call.8
  206.1 0.2 broadcast_multiply_fusion
  206.4 1.3 collective-permute-start.5
  207.7 4.8 %collective-permute-start.4 = (f32[256,32]{0,1:T(8,128)S(1)}, f32[256,32]{0,1:T(8,128)S(1)}, u32[]{:S(2)}, u32[]{:S(2)}) collective-permute-start(f32[256,32]{0,1:T(8,128)S(1)} %get-tuple-element.20), channel_id=1, source_target_pairs={{0,1},{1,2},{2,3},{3,4},{4,5},{5,6},{6,7},{8,9},{9,10},{10,11},{11... | collective-permute-start | bytes 98312 | tf_op jit(solution)/shard_map/ppermute | solution.py:18
  212.5 0.9 fusion.44
  213.4 0.7 collective-permute-done.4
  214.1 7.2 %all-gather.2 = f32[3072,32]{0,1:T(8,128)S(1)} all-gather(f32[768,32]{0,1:T(8,128)S(1)} %pad_maximum_fusion.2), channel_id=4, replica_groups=mesh['loop'=4,'inner'=8] {'loop'}, dimensions={0}, use_global_device_ids=true | all-gather | bytes 491520 | tf_op jit(solution)/shard_map/all_gather | solution.py:104
  221.3 2.8 convolution_multiply_fusion.2
  224.2 41.7 %psum.38 = f32[32,32]{0,1:T(8,128)S(1)} all-reduce(f32[32,32]{0,1:T(8,128)S(1)} %fusion.59), channel_id=1, replica_groups=mesh['loop'=4,'inner'=8] {'loop','inner'}, use_global_device_ids=true, to_apply=%region_8.11 | all-reduce | flops 1024 | bytes 8192 | tf_op jit(solution)/shard_map/psum | solution.py:108
  266.3 39.8 %psum.39 = f32[32,32]{0,1:T(8,128)S(1)} all-reduce(f32[32,32]{0,1:T(8,128)S(1)} %fusion.60), channel_id=1, replica_groups=mesh['loop'=4,'inner'=8] {'loop','inner'}, use_global_device_ids=true, to_apply=%region_9.12 | all-reduce | flops 1024 | bytes 8192 | tf_op jit(solution)/shard_map/psum | solution.py:112
  306.2 2.9 cholesky.81
  309.1 0.6 compare_reduce_fusion
  309.8 0.7 fusion.42
  310.4 2.4 custom-call.9
  312.9 0.2 convolution_bitcast_fusion
  313.1 0.6 pad_maximum_fusion.3
  313.8 0.7 copy.35
  (40 shorter events, 1.4 us)
Async XLA Ops:
  7.2 31.2 %copy-start = (bf16[1024,32]{0,1:T(8,128)(2,1)S(1)}, bf16[1024,32]{0,1:T(8,128)(2,1)}, u32[]{:S(2)}) copy-start(bf16[1024,32]{0,1:T(8,128)(2,1)} %param.10) | copy-start | bytes 196612
  7.2 31.2 %copy-start.2 = (bf16[256,1024]{1,0:T(8,128)(2,1)S(1)}, bf16[256,1024]{1,0:T(8,128)(2,1)}, u32[]{:S(2)}) copy-start(bf16[256,1024]{1,0:T(8,128)(2,1)} %param.7) | copy-start | bytes 1572868
  7.2 31.0 %copy-start.3 = (s32[8192]{0:T(1024)S(1)}, s32[8192]{0:T(1024)}, u32[]{:S(2)}) copy-start(s32[8192]{0:T(1024)} %param.8) | copy-start | bytes 98308
  7.2 80.9 %copy-start.4 = (s32[256,2]{0,1:T(2,128)S(1)}, s32[256,2]{0,1:T(2,128)}, u32[]{:S(2)}) copy-start(s32[256,2]{0,1:T(2,128)} %param.9) | copy-start | bytes 6148
  7.2 81.4 %all-gather.5.cloned.1.call-start = ((), (), s32[]{:S(2)}) async-start(), calls=%async_computation | async-start | bytes 7864320 | tf_op jit(solution)/shard_map/all_gather | solution.py:54
  7.3 17.1 %collective-permute-start.1 = (bf16[256,1024]{1,0:T(8,128)(2,1)}, bf16[256,1024]{1,0:T(8,128)(2,1)S(1)}, u32[]{:S(2)}, u32[]{:S(2)}) collective-permute-start(bf16[256,1024]{1,0:T(8,128)(2,1)} %param.7), channel_id=1, source_target_pairs={{1,0},{2,1},{3,2},{4,3},{5,4},{6,5},{7,6},{9,8},{10,9},{11,10},{12... | collective-permute-start | bytes 1572872 | tf_op jit(solution)/shard_map/ppermute | solution.py:20
  8.7 27.2 %collective-permute-start = (bf16[256,1024]{1,0:T(8,128)(2,1)}, bf16[256,1024]{1,0:T(8,128)(2,1)S(1)}, u32[]{:S(2)}, u32[]{:S(2)}) collective-permute-start(bf16[256,1024]{1,0:T(8,128)(2,1)} %param.7), channel_id=1, source_target_pairs={{0,1},{1,2},{2,3},{3,4},{4,5},{5,6},{6,7},{8,9},{9,10},{10,11},{11... | collective-permute-start | bytes 1572872 | tf_op jit(solution)/shard_map/ppermute | solution.py:18
  88.7 4.6 %copy-start.1 = (bf16[3072,1024]{1,0:T(8,128)(2,1)S(1)}, bf16[3072,1024]{1,0:T(8,128)(2,1)}, u32[]{:S(2)}) copy-start(bf16[3072,1024]{1,0:T(8,128)(2,1)} %all-gather.5.cloned.1.call-done) | copy-start | bytes 18874372
  100.3 6.1 %collective-permute-start.3 = (f32[256,32]{0,1:T(8,128)S(1)}, f32[256,32]{0,1:T(8,128)S(1)}, u32[]{:S(2)}, u32[]{:S(2)}) collective-permute-start(f32[256,32]{0,1:T(8,128)S(1)} %get-tuple-element.18), channel_id=1, source_target_pairs={{1,0},{2,1},{3,2},{4,3},{5,4},{6,5},{7,6},{9,8},{10,9},{11,10},{12... | collective-permute-start | bytes 98312 | tf_op jit(solution)/shard_map/ppermute | solution.py:20
  101.6 6.4 %collective-permute-start.2 = (f32[256,32]{0,1:T(8,128)S(1)}, f32[256,32]{0,1:T(8,128)S(1)}, u32[]{:S(2)}, u32[]{:S(2)}) collective-permute-start(f32[256,32]{0,1:T(8,128)S(1)} %get-tuple-element.18), channel_id=1, source_target_pairs={{0,1},{1,2},{2,3},{3,4},{4,5},{5,6},{6,7},{8,9},{9,10},{10,11},{11... | collective-permute-start | bytes 98312 | tf_op jit(solution)/shard_map/ppermute | solution.py:18
  206.4 7.0 %collective-permute-start.5 = (f32[256,32]{0,1:T(8,128)S(1)}, f32[256,32]{0,1:T(8,128)S(1)}, u32[]{:S(2)}, u32[]{:S(2)}) collective-permute-start(f32[256,32]{0,1:T(8,128)S(1)} %get-tuple-element.20), channel_id=1, source_target_pairs={{1,0},{2,1},{3,2},{4,3},{5,4},{6,5},{7,6},{9,8},{10,9},{11,10},{12... | collective-permute-start | bytes 98312 | tf_op jit(solution)/shard_map/ppermute | solution.py:20
  207.7 6.4 %collective-permute-start.4 = (f32[256,32]{0,1:T(8,128)S(1)}, f32[256,32]{0,1:T(8,128)S(1)}, u32[]{:S(2)}, u32[]{:S(2)}) collective-permute-start(f32[256,32]{0,1:T(8,128)S(1)} %get-tuple-element.20), channel_id=1, source_target_pairs={{0,1},{1,2},{2,3},{3,4},{4,5},{5,6},{6,7},{8,9},{9,10},{10,11},{11... | collective-permute-start | bytes 98312 | tf_op jit(solution)/shard_map/ppermute | solution.py:18
Sparse Core Ops, SparseCore 0:
  38.3 48.3 all-gather.4
where the time goes:
time: 323 us; the launch traced here: 321 us
  blocking collectives  219 us (68%)
  other arithmetic  27.5 us (9%)
  waiting for transfers between devices  24 us (7%)
  starting transfers between devices  19.2 us (6%)
  matrix products  15.9 us (5%)
  between operations  14.4 us (4%)
    psum x2, blocking collectives, local(): projected = lax.psum(local_gram(current, image), ('loop', 'inner'))  83.1 us
    psum x2, blocking collectives, local(): gram_total = lax.psum(local_gram(image, image), ('loop', 'inner'))  79.3 us
    psum x1, blocking collectives, local(): lax.psum(local_gram(start_block, start_block), ('loop', 'inner'))  42.3 us
    ppermute x3, starting transfers between devices, extended(): lax.ppermute(tail, axis, [(i, (i + 1) % count) for i in range(ends)])  15.1 us
    all_gather x2, blocking collectives, local(): vec_strip = lax.all_gather(vec_side[None], 'loop', axis=0, tiled=True)  14.3 us
    ppermute x3, waiting for transfers between devices, extended(): lax.ppermute(tail, axis, [(i, (i + 1) % count) for i in range(ends)])  13.8 us
    another operation x9, other arithmetic, finish(): lower_factor = jnp.linalg.cholesky(gram_total)  10.8 us
    ppermute x3, waiting for transfers between devices, extended(): lax.ppermute(head, axis, [((i + 1) % count, i) for i in range(ends)])  10.2 us
  transfers between devices with their start and end apart: 7, of which 4 were waited for; matrix products, arithmetic and copies ran while one was open for 3% of the time, Pallas kernels for 0%

commit v1 on v0

--- a/solution.py
+++ b/solution.py
@@ -92,7 +92,9 @@
     degree = jnp.sum(current_kernel(0), axis=1)
     inv_root = lax.rsqrt(degree)
     start_block = jnp.dot(snapshots, start_weights, preferred_element_type=jnp.float32)
-    start_total = lax.psum(local_gram(start_block, start_block), ("loop", "inner"))
+    start_total = jnp.sum(
+        lax.all_gather(local_gram(start_block, start_block), ("loop", "inner")), axis=0
+    )
     current, unused = finish(start_block, start_total)
     basis_blocks = [current]
     coefficients = []

time: 323 us -> 348 us (1.077)
  blocking collectives: 219 us -> 245 us
    all_gather x0 -> x1, blocking collectives: none -> 69.3 us  [local(): lax.all_gather(local_gram(start_block, start_block), ('loop', 'inner'))]
    psum x1 -> x0, blocking collectives: 42.3 us -> none  [local(): lax.psum(local_gram(start_block, start_block), ('loop', 'inner'))]
where the time goes in v1:
time: 348 us; the launch traced here: 347 us
  blocking collectives  245 us (70%)
  other arithmetic  27.5 us (8%)
  waiting for transfers between devices  23.9 us (7%)
  starting transfers between devices  18.9 us (5%)
  matrix products  15.9 us (5%)
  between operations  14.4 us (4%)
    psum x2, blocking collectives, local(): projected = lax.psum(local_gram(current, image), ('loop', 'inner'))  82 us
    psum x2, blocking collectives, local(): gram_total = lax.psum(local_gram(image, image), ('loop', 'inner'))  79.4 us
    all_gather x1, blocking collectives, local(): lax.all_gather(local_gram(start_block, start_block), ('loop', 'inner'))  69.3 us
    ppermute x3, starting transfers between devices, extended(): lax.ppermute(tail, axis, [(i, (i + 1) % count) for i in range(ends)])  14.9 us
    all_gather x2, blocking collectives, local(): vec_strip = lax.all_gather(vec_side[None], 'loop', axis=0, tiled=True)  13.9 us
    ppermute x3, waiting for transfers between devices, extended(): lax.ppermute(tail, axis, [(i, (i + 1) % count) for i in range(ends)])  13.8 us
    another operation x9, other arithmetic, finish(): lower_factor = jnp.linalg.cholesky(gram_total)  10.8 us
    ppermute x3, waiting for transfers between devices, extended(): lax.ppermute(head, axis, [((i + 1) % count, i) for i in range(ends)])  10.2 us
  transfers between devices with their start and end apart: 7, of which 4 were waited for; matrix products, arithmetic and copies ran while one was open for 3% of the time, Pallas kernels for 0%

profile of v1, /device:TPU:0, one launch (start us, length us, event | category | flops | bytes accessed | tf_op | source)
XLA Modules:
  0.0 346.6 jit_solution(15581234949017729407)
XLA Ops:
  7.3 1.4 collective-permute-start.1
  8.7 5.5 %collective-permute-start = (bf16[256,1024]{1,0:T(8,128)(2,1)}, bf16[256,1024]{1,0:T(8,128)(2,1)S(1)}, u32[]{:S(2)}, u32[]{:S(2)}) collective-permute-start(bf16[256,1024]{1,0:T(8,128)(2,1)} %param.7), channel_id=1, source_target_pairs={{0,1},{1,2},{2,3},{3,4},{4,5},{5,6},{6,7},{8,9},{9,10},{10,11},{11... | collective-permute-start | bytes 1572872 | tf_op jit(solution)/shard_map/ppermute | solution.py:18
  14.2 10.2 %collective-permute-done.1 = bf16[256,1024]{1,0:T(8,128)(2,1)S(1)} collective-permute-done((bf16[256,1024]{1,0:T(8,128)(2,1)}, bf16[256,1024]{1,0:T(8,128)(2,1)S(1)}, u32[]{:S(2)}, u32[]{:S(2)}) %collective-permute-start.1) | collective-permute-done | bytes 524320 | tf_op jit(solution)/shard_map/ppermute | solution.py:20
  24.4 11.5 %collective-permute-done = bf16[256,1024]{1,0:T(8,128)(2,1)S(1)} collective-permute-done((bf16[256,1024]{1,0:T(8,128)(2,1)}, bf16[256,1024]{1,0:T(8,128)(2,1)S(1)}, u32[]{:S(2)}, u32[]{:S(2)}) %collective-permute-start) | collective-permute-done | bytes 524320 | tf_op jit(solution)/shard_map/ppermute | solution.py:18
  35.9 2.3 pad_maximum_fusion
  38.4 0.2 fusion.55
  38.6 0.2 fusion.56
  38.8 69.3 %all-gather = f32[1024,32]{1,0:T(8,128)S(1)} all-gather(f32[32,32]{1,0:T(8,128)S(1)} %fusion.56), channel_id=2, replica_groups=mesh['loop'=4,'inner'=8] {'loop','inner'}, dimensions={0}, use_global_device_ids=true | all-gather | bytes 135168 | tf_op jit(solution)/shard_map/all_gather | solution.py:96
  108.2 2.9 cholesky.59
  111.2 0.6 compare_reduce_fusion.2
  111.8 0.7 fusion.35
  112.5 2.4 custom-call.7
  115.0 0.2 multiply_reduce_fusion.1
  115.2 0.3 fusion.20
  115.4 0.3 fusion.9
  115.7 4.2 %multiply_reduce_fusion = f32[3072]{0:T(1024)S(1)} fusion(bf16[3072,1024]{1,0:T(8,128)(2,1)} %all-gather.6.cloned.1.call-done), kind=kLoop, calls=%fused_computation | loop fusion | flops 9434112 | bytes 6303744 | tf_op jit(solution)/shard_map/reduce_sum | solution.py:82
  120.0 0.4 copy-done.1
  120.3 4.0 %fusion.4 = f32[256,3072]{1,0:T(8,128)} fusion(bf16[3072,1024]{1,0:T(8,128)(2,1)S(1)} %copy-done.1, bf16[256,1024]{1,0:T(8,128)(2,1)S(1)} %copy-done.2, f32[3072]{0:T(1024)S(1)} %multiply_reduce_fusion, f32[256]{0:T(256)S(1)} %multiply_reduce_fusion.1), kind=kOutput, calls=%fused_computation.7 | convolution fusion | flops 1614544896 | bytes 9974784 | tf_op jit(solution)/shard_map/dot_general | solution.py:83
  124.3 2.8 fusion.52
  127.2 0.2 broadcast_multiply_fusion.1
  127.4 1.3 collective-permute-start.3
  128.7 4.5 %collective-permute-start.2 = (f32[256,32]{0,1:T(8,128)S(1)}, f32[256,32]{0,1:T(8,128)S(1)}, u32[]{:S(2)}, u32[]{:S(2)}) collective-permute-start(f32[256,32]{0,1:T(8,128)S(1)} %get-tuple-element.20), channel_id=1, source_target_pairs={{0,1},{1,2},{2,3},{3,4},{4,5},{5,6},{6,7},{8,9},{9,10},{10,11},{11... | collective-permute-start | bytes 98312 | tf_op jit(solution)/shard_map/ppermute | solution.py:18
  133.3 1.6 collective-permute-done.2
  134.8 6.7 %all-gather.2 = f32[3072,32]{0,1:T(8,128)S(1)} all-gather(f32[768,32]{0,1:T(8,128)S(1)} %pad_maximum_fusion.1), channel_id=4, replica_groups=mesh['loop'=4,'inner'=8] {'loop'}, dimensions={0}, use_global_device_ids=true | all-gather | bytes 491520 | tf_op jit(solution)/shard_map/all_gather | solution.py:106
  141.5 2.8 convolution_multiply_fusion.3
  144.5 40.4 %psum.28 = f32[32,32]{0,1:T(8,128)S(1)} all-reduce(f32[32,32]{0,1:T(8,128)S(1)} %fusion.57), channel_id=1, replica_groups=mesh['loop'=4,'inner'=8] {'loop','inner'}, use_global_device_ids=true, to_apply=%region_6.9 | all-reduce | flops 1024 | bytes 8192 | tf_op jit(solution)/shard_map/psum | solution.py:110
  185.2 39.8 %psum.29 = f32[32,32]{0,1:T(8,128)S(1)} all-reduce(f32[32,32]{0,1:T(8,128)S(1)} %fusion.58), channel_id=1, replica_groups=mesh['loop'=4,'inner'=8] {'loop','inner'}, use_global_device_ids=true, to_apply=%region_7.10 | all-reduce | flops 1024 | bytes 8192 | tf_op jit(solution)/shard_map/psum | solution.py:114
  225.1 2.9 cholesky.70
  228.0 0.6 compare_reduce_fusion.1
  228.7 0.7 fusion.43
  229.3 2.4 custom-call.8
  231.8 0.2 broadcast_multiply_fusion
  232.0 1.3 collective-permute-start.5
  233.3 4.8 %collective-permute-start.4 = (f32[256,32]{0,1:T(8,128)S(1)}, f32[256,32]{0,1:T(8,128)S(1)}, u32[]{:S(2)}, u32[]{:S(2)}) collective-permute-start(f32[256,32]{0,1:T(8,128)S(1)} %get-tuple-element.22), channel_id=1, source_target_pairs={{0,1},{1,2},{2,3},{3,4},{4,5},{5,6},{6,7},{8,9},{9,10},{10,11},{11... | collective-permute-start | bytes 98312 | tf_op jit(solution)/shard_map/ppermute | solution.py:18
  238.2 0.9 fusion.44
  239.0 0.7 collective-permute-done.4
  239.7 7.2 %all-gather.3 = f32[3072,32]{0,1:T(8,128)S(1)} all-gather(f32[768,32]{0,1:T(8,128)S(1)} %pad_maximum_fusion.2), channel_id=5, replica_groups=mesh['loop'=4,'inner'=8] {'loop'}, dimensions={0}, use_global_device_ids=true | all-gather | bytes 491520 | tf_op jit(solution)/shard_map/all_gather | solution.py:106
  246.9 2.8 convolution_multiply_fusion.2
  249.7 0.2 fusion.59
  249.9 41.6 %psum.30 = f32[32,32]{0,1:T(8,128)S(1)} all-reduce(f32[32,32]{0,1:T(8,128)S(1)} %fusion.59), channel_id=1, replica_groups=mesh['loop'=4,'inner'=8] {'loop','inner'}, use_global_device_ids=true, to_apply=%region_8.11 | all-reduce | flops 1024 | bytes 8192 | tf_op jit(solution)/shard_map/psum | solution.py:110
  291.9 39.5 %psum.31 = f32[32,32]{0,1:T(8,128)S(1)} all-reduce(f32[32,32]{0,1:T(8,128)S(1)} %fusion.60), channel_id=1, replica_groups=mesh['loop'=4,'inner'=8] {'loop','inner'}, use_global_device_ids=true, to_apply=%region_9.12 | all-reduce | flops 1024 | bytes 8192 | tf_op jit(solution)/shard_map/psum | solution.py:114
  331.5 2.9 cholesky.81
  334.4 0.6 compare_reduce_fusion
  335.1 0.7 fusion.42
  335.7 2.4 custom-call.9
  338.2 0.2 convolution_bitcast_fusion
  338.4 0.6 pad_maximum_fusion.3
  339.1 0.7 copy.41
  (41 shorter events, 1.5 us)
Async XLA Ops:
  7.2 31.2 %copy-start = (bf16[1024,32]{0,1:T(8,128)(2,1)S(1)}, bf16[1024,32]{0,1:T(8,128)(2,1)}, u32[]{:S(2)}) copy-start(bf16[1024,32]{0,1:T(8,128)(2,1)} %param.10) | copy-start | bytes 196612
  7.2 31.2 %copy-start.2 = (bf16[256,1024]{1,0:T(8,128)(2,1)S(1)}, bf16[256,1024]{1,0:T(8,128)(2,1)}, u32[]{:S(2)}) copy-start(bf16[256,1024]{1,0:T(8,128)(2,1)} %param.7) | copy-start | bytes 1572868
  7.2 31.0 %copy-start.3 = (s32[8192]{0:T(1024)S(1)}, s32[8192]{0:T(1024)}, u32[]{:S(2)}) copy-start(s32[8192]{0:T(1024)} %param.8) | copy-start | bytes 98308
  7.2 107.9 %copy-start.4 = (s32[256,2]{0,1:T(2,128)S(1)}, s32[256,2]{0,1:T(2,128)}, u32[]{:S(2)}) copy-start(s32[256,2]{0,1:T(2,128)} %param.9) | copy-start | bytes 6148
  7.2 108.5 %all-gather.6.cloned.1.call-start = ((), (), s32[]{:S(2)}) async-start(), calls=%async_computation | async-start | bytes 7864320 | tf_op jit(solution)/shard_map/all_gather | solution.py:54
  7.3 17.1 %collective-permute-start.1 = (bf16[256,1024]{1,0:T(8,128)(2,1)}, bf16[256,1024]{1,0:T(8,128)(2,1)S(1)}, u32[]{:S(2)}, u32[]{:S(2)}) collective-permute-start(bf16[256,1024]{1,0:T(8,128)(2,1)} %param.7), channel_id=1, source_target_pairs={{1,0},{2,1},{3,2},{4,3},{5,4},{6,5},{7,6},{9,8},{10,9},{11,10},{12... | collective-permute-start | bytes 1572872 | tf_op jit(solution)/shard_map/ppermute | solution.py:20
  8.7 27.2 %collective-permute-start = (bf16[256,1024]{1,0:T(8,128)(2,1)}, bf16[256,1024]{1,0:T(8,128)(2,1)S(1)}, u32[]{:S(2)}, u32[]{:S(2)}) collective-permute-start(bf16[256,1024]{1,0:T(8,128)(2,1)} %param.7), channel_id=1, source_target_pairs={{0,1},{1,2},{2,3},{3,4},{4,5},{5,6},{6,7},{8,9},{9,10},{10,11},{11... | collective-permute-start | bytes 1572872 | tf_op jit(solution)/shard_map/ppermute | solution.py:18
  115.7 4.6 %copy-start.1 = (bf16[3072,1024]{1,0:T(8,128)(2,1)S(1)}, bf16[3072,1024]{1,0:T(8,128)(2,1)}, u32[]{:S(2)}) copy-start(bf16[3072,1024]{1,0:T(8,128)(2,1)} %all-gather.6.cloned.1.call-done) | copy-start | bytes 18874372
  127.4 5.9 %collective-permute-start.3 = (f32[256,32]{0,1:T(8,128)S(1)}, f32[256,32]{0,1:T(8,128)S(1)}, u32[]{:S(2)}, u32[]{:S(2)}) collective-permute-start(f32[256,32]{0,1:T(8,128)S(1)} %get-tuple-element.20), channel_id=1, source_target_pairs={{1,0},{2,1},{3,2},{4,3},{5,4},{6,5},{7,6},{9,8},{10,9},{11,10},{12... | collective-permute-start | bytes 98312 | tf_op jit(solution)/shard_map/ppermute | solution.py:20
  128.7 6.1 %collective-permute-start.2 = (f32[256,32]{0,1:T(8,128)S(1)}, f32[256,32]{0,1:T(8,128)S(1)}, u32[]{:S(2)}, u32[]{:S(2)}) collective-permute-start(f32[256,32]{0,1:T(8,128)S(1)} %get-tuple-element.20), channel_id=1, source_target_pairs={{0,1},{1,2},{2,3},{3,4},{4,5},{5,6},{6,7},{8,9},{9,10},{10,11},{11... | collective-permute-start | bytes 98312 | tf_op jit(solution)/shard_map/ppermute | solution.py:18
  232.0 7.0 %collective-permute-start.5 = (f32[256,32]{0,1:T(8,128)S(1)}, f32[256,32]{0,1:T(8,128)S(1)}, u32[]{:S(2)}, u32[]{:S(2)}) collective-permute-start(f32[256,32]{0,1:T(8,128)S(1)} %get-tuple-element.22), channel_id=1, source_target_pairs={{1,0},{2,1},{3,2},{4,3},{5,4},{6,5},{7,6},{9,8},{10,9},{11,10},{12... | collective-permute-start | bytes 98312 | tf_op jit(solution)/shard_map/ppermute | solution.py:20
  233.3 6.4 %collective-permute-start.4 = (f32[256,32]{0,1:T(8,128)S(1)}, f32[256,32]{0,1:T(8,128)S(1)}, u32[]{:S(2)}, u32[]{:S(2)}) collective-permute-start(f32[256,32]{0,1:T(8,128)S(1)} %get-tuple-element.22), channel_id=1, source_target_pairs={{0,1},{1,2},{2,3},{3,4},{4,5},{5,6},{6,7},{8,9},{9,10},{10,11},{11... | collective-permute-start | bytes 98312 | tf_op jit(solution)/shard_map/ppermute | solution.py:18
Sparse Core Ops, SparseCore 0:
  38.3 48.8 all-gather.5
